TPU v7x, 32 devices: a whole 2x2x4 slice. The times are simulated.
32 devices in a mesh: gx: 4 (over y, x), gy: 4 (over z), gz: 2 (over core).
Axes of the slice: x: 2, y: 2, z: 4, core: 2. Of those that a mesh axis runs over, the one named last changes fastest.
Arguments:
- provisional: float32 [9, 128, 64, 256], P(None, 'gx', 'gy', 'gz'), may hold values from -6 to 6
- cut_flag: int32 [128, 64, 256], P('gx', 'gy', 'gz'), may hold values from 0 to 1, as said below
- cut_code: int32 [128, 64, 256], P('gx', 'gy', 'gz'), may hold values from 0 to 134217727
- volume_level: int32 [128, 64, 256], P('gx', 'gy', 'gz'), may hold values from 1 to 256
- area_level: int32 [128, 64, 256], P('gx', 'gy', 'gz'), may hold values from 64 to 256
Outputs:
- redistributed: float32 [9, 128, 64, 256], P(None, 'gx', 'gy', 'gz')
- species_change: float32 [9], replicated
Inputs may be any that keep to these rules, and one draw needn't show every extreme that they name: cut_flag marks the cells crossed by one closed embedded surface.
All inputs are finite; a program needn't handle non-finite values.
Results may differ from a plain program's by a relative error of at most 0.00002.
Values sent between devices are 32-bit elements; how exact they have to be, the bound alone decides.
A program may use at most 128 MiB of HBM per device.

v0:
```python
import math

import jax
import jax.numpy as jnp
from jax import lax
from jax.sharding import PartitionSpec as P

CENTER = 8192
OFFSETS = [(a, b, c) for a in (-1, 0, 1) for b in (-1, 0, 1) for c in (-1, 0, 1)]


def padded(cells, sides, width):
    for axis, dim in sides:
        count = lax.axis_size(axis)
        ends = count - 1
        head = lax.slice_in_dim(cells, 0, width, axis=dim)
        tail = lax.slice_in_dim(cells, cells.shape[dim] - width, cells.shape[dim], axis=dim)
        cells = jnp.concatenate(
            [
                lax.ppermute(tail, axis, [(i, (i + 1) % count) for i in range(ends)]),
                cells,
                lax.ppermute(head, axis, [((i + 1) % count, i) for i in range(ends)]),
            ],
            axis=dim,
        )
    return cells


def window(values, a, b, c, margin, border):
    extent_x = values.shape[-3] - 2 * border + 2 * margin
    extent_y = values.shape[-2] - 2 * border + 2 * margin
    extent_z = values.shape[-1] - 2 * border + 2 * margin
    start_x = border - margin + a
    start_y = border - margin + b
    start_z = border - margin + c
    return values[
        ...,
        start_x : start_x + extent_x,
        start_y : start_y + extent_y,
        start_z : start_z + extent_z,
    ]


def member(codes, position):
    return (codes >> position & 1).astype(jnp.float32)


def per_device(provisional, cut_flag, cut_code, volume_level, area_level):
    is_cut = cut_flag == 1
    stacked = jnp.stack(
        [
            jnp.where(is_cut, cut_code | CENTER, CENTER),
            jnp.where(is_cut, volume_level, 256),
            jnp.where(is_cut, area_level, 256),
        ]
    )
    border = 2
    grown = padded(stacked, (("gx", 1), ("gy", 2), ("gz", 3)), border)
    code_all = grown[0] | CENTER
    volume_all = grown[1].astype(jnp.float32) / 256.0
    face_all = grown[2].astype(jnp.float32) / 256.0
    margin = border - 1
    counted = jnp.zeros(window(code_all, 0, 0, 0, margin, border).shape, jnp.float32)
    for position, (a, b, c) in enumerate(OFFSETS):
        counted = counted + member(window(code_all, -a, -b, -c, margin, border), position)
    volume_near = window(volume_all, 0, 0, 0, margin, border)
    face_near = window(face_all, 0, 0, 0, margin, border)
    weights = volume_near / counted
    portions = volume_near * face_near / counted
    scaling = window(face_all, 0, 0, 0, 0, border) / window(counted, 0, 0, 0, 0, margin)
    volume_mid = window(volume_all, 0, 0, 0, 0, border)
    carried = padded(
        window(weights, 0, 0, 0, 0, 1)[None] * provisional, (("gx", 1), ("gy", 2), ("gz", 3)), 1
    )
    carry_border = 1
    inner_margin = 0
    code_inner = window(code_all, 0, 0, 0, inner_margin, border)
    beyond = (window(grown[1], 0, 0, 0, inner_margin, border) == 0).astype(jnp.float32)
    amounts = jnp.zeros(window(carried, 0, 0, 0, inner_margin, carry_border).shape, jnp.float32)
    gathered = jnp.zeros(code_inner.shape, jnp.float32)
    for position, (a, b, c) in enumerate(OFFSETS):
        present = member(code_inner, position)
        amounts = amounts + present * window(carried, a, b, c, inner_margin, carry_border)
        gathered = gathered + present * window(portions, a, b, c, inner_margin, margin)
    quotas = amounts / (gathered + beyond)
    quotas = padded(quotas, (("gx", 1), ("gy", 2), ("gz", 3)), 1)
    summed = jnp.zeros(provisional.shape, jnp.float32)
    for position, (a, b, c) in enumerate(OFFSETS):
        summed = summed + member(window(code_all, -a, -b, -c, 0, border), position) * window(
            quotas, -a, -b, -c, 0, 1
        )
    redistributed = scaling * summed
    cell_count = (
        provisional.shape[1]
        * provisional.shape[2]
        * provisional.shape[3]
        * lax.axis_size("gx")
        * lax.axis_size("gy")
        * lax.axis_size("gz")
    )
    local_sums = jnp.sum(volume_mid[None] * redistributed, axis=(1, 2, 3))
    species_change = lax.psum(local_sums, ("gx", "gy", "gz")) / math.sqrt(cell_count)
    return (redistributed, species_change)


def solution(mesh):
    in_specs = (
        P(None, "gx", "gy", "gz"),
        P("gx", "gy", "gz"),
        P("gx", "gy", "gz"),
        P("gx", "gy", "gz"),
        P("gx", "gy", "gz"),
    )
    out_specs = (P(None, "gx", "gy", "gz"), P())
    return jax.shard_map(
        per_device, mesh=mesh, in_specs=in_specs, out_specs=out_specs, check_vma=False
    )
```

profile of v0, /device:TPU:0, one launch (start us, length us, event | category | flops | bytes accessed | tf_op | source)
XLA Modules:
  0.0 276.7 jit_solution(5008713613444649050)
XLA Ops:
  2.8 4.9 %collective-permute-start = (s32[3,2,16,128]{3,2,1,0:T(8,128)S(1)}, s32[3,2,16,128]{3,2,1,0:T(8,128)S(1)}, u32[]{:S(2)}, u32[]{:S(2)}) collective-permute-start(s32[3,2,16,128]{3,2,1,0:T(8,128)S(1)} %get-tuple-element.91), channel_id=1, source_target_pairs={{0,8},{8,16},{16,24},{1,9},{9,17},{17,25},{2,10},{10,18},{18,26},{... | collective-permute-start | bytes 147464 | tf_op jit(solution)/shard_map/ppermute | solution.py:20
  7.7 1.3 collective-permute-start.1
  9.4 4.2 %collective-permute-done.1 = s32[3,2,16,128]{3,2,1,0:T(8,128)S(1)} collective-permute-done((s32[3,2,16,128]{3,2,1,0:T(8,128)S(1)}, s32[3,2,16,128]{3,2,1,0:T(8,128)S(1)}, u32[]{:S(2)}, u32[]{:S(2)}) %collective-permute-start.1) | collective-permute-done | bytes 49184 | tf_op jit(solution)/shard_map/ppermute | solution.py:22
  13.8 3.5 %collective-permute-start.2 = (s32[3,36,2,128]{3,2,1,0:T(2,128)S(1)}, s32[3,36,2,128]{3,2,1,0:T(2,128)S(1)}, u32[]{:S(2)}, u32[]{:S(2)}) collective-permute-start(s32[3,36,2,128]{3,2,1,0:T(2,128)S(1)} %get-tuple-element.87), channel_id=1, source_target_pairs={{0,2},{2,4},{4,6},{1,3},{3,5},{5,7},{8,10},{10,12},{12,14},{9,11},... | collective-permute-start | bytes 331784 | tf_op jit(solution)/shard_map/ppermute | solution.py:20
  17.3 1.3 collective-permute-start.3
  19.6 4.3 %collective-permute-done.3 = s32[3,36,2,128]{3,2,1,0:T(2,128)S(1)} collective-permute-done((s32[3,36,2,128]{3,2,1,0:T(2,128)S(1)}, s32[3,36,2,128]{3,2,1,0:T(2,128)S(1)}, u32[]{:S(2)}, u32[]{:S(2)}) %collective-permute-start.3) | collective-permute-done | bytes 110624 | tf_op jit(solution)/shard_map/ppermute | solution.py:22
  26.3 1.3 collective-permute-start.4
  28.2 1.3 collective-permute-start.5
  30.1 1.3 collective-permute-done.5
  31.4 1.5 copy.196
  32.9 4.2 %pad_add_fusion = s32[3,36,20,132]{3,2,1,0:T(8,128)S(1)} fusion(s32[3,36,20,2]{3,2,1,0:T(8,128)S(1)} %copy.196, s32[3,36,2,128]{3,2,1,0:T(2,128)} %copy-done.4, s32[3,2,16,128]{3,2,1,0:T(8,128)} %copy-done.6, s32[1,32,16,128]{3,2,1,0:T(8,128)S(1)} %get-tuple-element.94, s32[1,32,16,128]{3,2,1,0:T(8,128)S(1)} %get-tuple-element.93, ...), kind=kLoop, calls=%fused_computation.10 | loop fusion | flops 2280960 | bytes 2280960 | tf_op jit(solution)/shard_map/concatenate | solution.py:18
  37.6 3.0 %fusion.220 = (f32[32,16,128]{2,1,0:T(8,128)}, f32[32,16,128]{2,1,0:T(8,128)}, f32[32,16,128]{2,1,0:T(8,128)}, f32[32,16,128]{2,1,0:T(8,128)}, f32[32,16,128]{2,...) fusion(s32[36,20,132]{2,1,0:T(8,128)S(1)} %get-tuple-element.19), kind=kLoop, calls=%fused_computation.373 | loop fusion | flops 3735552 | bytes 5505024 | tf_op jit(solution)/shard_map/convert_element_type | solution.py:45
  40.6 4.8 %fusion.61 = (f32[34,18,130]{2,1,0:T(8,128)S(1)}, f32[34,18,130]{2,1,0:T(8,128)S(1)}) fusion(f32[36,20,132]{2,1,0:T(8,128)S(1)} %fusion.60, f32[36,20,132]{2,1,0:T(8,128)S(1)} %convert_multiply_fusion, s32[36,20,132]{2,1,0:T(8,128)S(1)} %get-tuple-element.19), kind=kLoop, calls=%fused_computation.132 | loop fusion | flops 8672040 | bytes 9865440 | tf_op jit(solution)/shard_map/div | solution.py:69
  46.6 4.3 %collective-permute-start.6 = (f32[9,1,16,128]{3,2,1,0:T(8,128)S(1)}, f32[9,1,16,128]{3,2,1,0:T(8,128)S(1)}, u32[]{:S(2)}, u32[]{:S(2)}) collective-permute-start(f32[9,1,16,128]{3,2,1,0:T(8,128)S(1)} %get-tuple-element.30), channel_id=1, source_target_pairs={{0,8},{8,16},{16,24},{1,9},{9,17},{17,25},{2,10},{10,18},{18,26},{... | collective-permute-start | bytes 221192 | tf_op jit(solution)/shard_map/ppermute | solution.py:20
  50.9 1.3 collective-permute-start.7
  52.2 2.3 fusion.193
  54.5 3.1 %fusion.191 = (f32[32,16,128]{2,1,0:T(8,128)}, f32[32,16,128]{2,1,0:T(8,128)}, f32[32,16,128]{2,1,0:T(8,128)}, f32[32,16,128]{2,1,0:T(8,128)}, f32[32,16,128]{2,...) fusion(s32[36,20,132]{2,1,0:T(8,128)S(1)} %get-tuple-element.19), kind=kLoop, calls=%fused_computation.314 | loop fusion | flops 3735552 | bytes 8126464 | tf_op jit(solution)/shard_map/convert_element_type | solution.py:45
  57.9 1.3 collective-permute-start.9
  59.2 4.7 %collective-permute-start.8 = (f32[9,34,1,128]{3,1,2,0:T(8,128)S(1)}, f32[9,34,1,128]{3,1,2,0:T(8,128)S(1)}, u32[]{:S(2)}, u32[]{:S(2)}) collective-permute-start(f32[9,34,1,128]{3,1,2,0:T(8,128)S(1)} %copy.197), channel_id=1, source_target_pairs={{0,2},{2,4},{4,6},{1,3},{3,5},{5,7},{8,10},{10,12},{12,14},{9,11},... | collective-permute-start | bytes 470024 | tf_op jit(solution)/shard_map/ppermute | solution.py:20
  63.9 3.0 %fusion.189 = (f32[32,16,128]{2,1,0:T(8,128)}, f32[32,16,128]{2,1,0:T(8,128)}, f32[32,16,128]{2,1,0:T(8,128)}, f32[32,16,128]{2,1,0:T(8,128)}, f32[32,16,128]{2,...) fusion(s32[36,20,132]{2,1,0:T(8,128)S(1)} %get-tuple-element.19), kind=kLoop, calls=%fused_computation.311 | loop fusion | flops 2949120 | bytes 7864320 | tf_op jit(solution)/shard_map/convert_element_type | solution.py:45
  68.4 4.2 %fusion.224 = (f32[9,34,18,1]{3,2,1,0:T(8,128)}, f32[9,34,18,1]{3,2,1,0:T(8,128)}) fusion(f32[9,34,18,128]{3,2,1,0:T(8,128)S(1)} %pad_maximum_fusion.2), kind=kLoop, calls=%fused_computation.422 | loop fusion | bytes 88128 | tf_op jit(solution)/shard_map/slice | solution.py:17
  72.6 3.5 %copy.201 = f32[9,34,18,1]{1,2,3,0:T(8,128)S(1)} copy(f32[9,34,18,1]{3,2,1,0:T(8,128)} %get-tuple-element.12) | data formatting | bytes 44064 | tf_op jit(solution)/shard_map/slice | solution.py:17
  76.1 3.5 %copy.204 = f32[9,34,18,1]{1,2,3,0:T(8,128)S(1)} copy(f32[9,34,18,1]{3,2,1,0:T(8,128)} %get-tuple-element.13) | data formatting | bytes 44064 | tf_op jit(solution)/shard_map/slice | solution.py:16
  79.7 1.3 collective-permute-start.11
  81.0 3.7 %collective-permute-start.10 = (f32[9,34,18,1]{1,2,3,0:T(8,128)S(1)}, f32[9,34,18,1]{1,2,3,0:T(8,128)}, u32[]{:S(2)}, u32[]{:S(2)}) collective-permute-start(f32[9,34,18,1]{1,2,3,0:T(8,128)S(1)} %copy.201), channel_id=1, source_target_pairs={{0,1},{2,3},{4,5},{6,7},{8,9},{10,11},{12,13},{14,15},{16,17},{18,... | collective-permute-start | bytes 66104 | tf_op jit(solution)/shard_map/ppermute | solution.py:20
  84.7 3.7 %maximum_maximum_fusion.2 = (f32[9,34,17,128]{3,2,1,0:T(8,128)}, f32[9,34,17,128]{3,2,1,0:T(8,128)}) fusion(f32[9,1,16,128]{3,2,1,0:T(8,128)S(1)} %collective-permute-done.7, f32[9,32,16,128]{3,2,1,0:T(8,128)S(1)} %broadcast_multiply_fusion, f32[9,1,16,128]{3,2,1,0:T(8,128)S(1)} %collective-permute-done.6, f32[9,34,1,128]{3,2,1,0:T(1,128)S(1)} %copy.199, ...), kind=kLoop, calls=%fused_computation.5 | loop fusion | flops 3995136 | bytes 8146944 | tf_op jit(solution)/shard_map/concatenate | solution.py:18
  88.4 3.9 %copy.202 = f32[9,34,18,1]{3,2,1,0:T(8,128)} copy(f32[9,34,18,1]{1,2,3,0:T(8,128)} %collective-permute-done.10) | data formatting | bytes 44064 | tf_op jit(solution)/shard_map/ppermute | solution.py:20
  92.3 3.2 %copy.205 = f32[9,34,18,1]{3,2,1,0:T(8,128)} copy(f32[9,34,18,1]{1,2,3,0:T(8,128)S(1)} %collective-permute-done.11) | data formatting | bytes 44064 | tf_op jit(solution)/shard_map/ppermute | solution.py:22
  95.5 10.9 %maximum_maximum_fusion = (f32[9,34,18,129]{3,2,1,0:T(8,128)S(1)}, f32[9,34,18,129]{3,2,1,0:T(8,128)}) fusion(f32[9,34,1,128]{3,2,1,0:T(1,128)S(1)} %copy.200, f32[9,1,16,128]{3,2,1,0:T(8,128)S(1)} %collective-permute-done.7, f32[9,32,16,128]{3,2,1,0:T(8,128)} %copy-done.1, f32[9,1,16,128]{3,2,1,0:T(8,128)S(1)} %collective-permute-done.6, ...), kind=kLoop, calls=%fused_computation | loop fusion | flops 7105320 | bytes 8548416 | tf_op jit(solution)/shard_map/concatenate | solution.py:18
  106.4 36.9 %fusion.30 = f32[9,32,16,128]{3,2,1,0:T(8,128)} fusion(f32[9,34,18,129]{3,2,1,0:T(8,128)} %get-tuple-element.17, f32[9,34,17,128]{3,2,1,0:T(8,128)} %get-tuple-element.25, f32[9,34,18,129]{3,2,1,0:T(8,128)S(1)} %get-tuple-element.16, f32[9,1,16,128]{3,2,1,0:T(8,128)S(1)} %collective-permute-done.7, f32[9,32,16,128]{3,2,1,0:T(8,128)} %copy-done.1, ...), kind=kLoop, calls=%fused_computation.68 | loop fusion | flops 33030144 | bytes 68829184 | tf_op jit(solution)/shard_map/div | solution.py:85
  144.3 4.4 %collective-permute-start.12 = (f32[9,1,16,128]{3,2,1,0:T(8,128)S(1)}, f32[9,1,16,128]{3,2,1,0:T(8,128)S(1)}, u32[]{:S(2)}, u32[]{:S(2)}) collective-permute-start(f32[9,1,16,128]{3,2,1,0:T(8,128)S(1)} %get-tuple-element.28), channel_id=1, source_target_pairs={{0,8},{8,16},{16,24},{1,9},{9,17},{17,25},{2,10},{10,18},{18,26},{... | collective-permute-start | bytes 221192 | tf_op jit(solution)/shard_map/ppermute | solution.py:20
  148.7 1.3 collective-permute-start.13
  150.7 4.3 %collective-permute-done.13 = f32[9,1,16,128]{3,2,1,0:T(8,128)S(1)} collective-permute-done((f32[9,1,16,128]{3,2,1,0:T(8,128)S(1)}, f32[9,1,16,128]{3,2,1,0:T(8,128)S(1)}, u32[]{:S(2)}, u32[]{:S(2)}) %collective-permute-start.13) | collective-permute-done | bytes 73760 | tf_op jit(solution)/shard_map/ppermute | solution.py:22
  155.0 1.9 pad_maximum_fusion.12
  156.9 1.3 collective-permute-start.15
  158.2 5.2 %collective-permute-start.14 = (f32[9,34,1,128]{3,1,2,0:T(8,128)S(1)}, f32[9,34,1,128]{3,1,2,0:T(8,128)S(1)}, u32[]{:S(2)}, u32[]{:S(2)}) collective-permute-start(f32[9,34,1,128]{3,1,2,0:T(8,128)S(1)} %copy.207), channel_id=1, source_target_pairs={{0,2},{2,4},{4,6},{1,3},{3,5},{5,7},{8,10},{10,12},{12,14},{9,11},... | collective-permute-start | bytes 470024 | tf_op jit(solution)/shard_map/ppermute | solution.py:20
  163.5 2.0 slice.847
  167.1 4.4 %fusion.223 = (f32[9,34,18,1]{3,2,1,0:T(8,128)}, f32[9,34,18,1]{3,2,1,0:T(8,128)}) fusion(f32[9,34,18,128]{3,2,1,0:T(8,128)S(1)} %pad_maximum_fusion.4), kind=kLoop, calls=%fused_computation.421 | loop fusion | bytes 88128 | tf_op jit(solution)/shard_map/slice | solution.py:16
  171.4 3.5 %copy.211 = f32[9,34,18,1]{1,2,3,0:T(8,128)S(1)} copy(f32[9,34,18,1]{3,2,1,0:T(8,128)} %get-tuple-element.10) | data formatting | bytes 44064 | tf_op jit(solution)/shard_map/slice | solution.py:16
  175.0 3.5 %copy.214 = f32[9,34,18,1]{1,2,3,0:T(8,128)S(1)} copy(f32[9,34,18,1]{3,2,1,0:T(8,128)} %get-tuple-element.11) | data formatting | bytes 44064 | tf_op jit(solution)/shard_map/slice | solution.py:17
  178.5 1.3 collective-permute-start.17
  179.8 1.3 collective-permute-start.16
  181.1 3.8 %pad_maximum_fusion.5 = (f32[9,34,17,128]{3,2,1,0:T(8,128)}, f32[9,34,17,128]{3,2,1,0:T(8,128)}) fusion(f32[9,34,1,128]{3,2,1,0:T(1,128)S(1)} %copy.210, f32[9,1,16,128]{3,2,1,0:T(8,128)S(1)} %collective-permute-done.13, f32[9,32,16,128]{3,2,1,0:T(8,128)S(1)} %copy-done, f32[9,1,16,128]{3,2,1,0:T(8,128)S(1)} %collective-permute-done.12, ...), kind=kLoop, calls=%fused_computation.8 | loop fusion | flops 3995136 | bytes 8146944 | tf_op jit(solution)/shard_map/concatenate | solution.py:18
  185.0 4.0 %copy.212 = f32[9,34,18,1]{3,2,1,0:T(8,128)} copy(f32[9,34,18,1]{1,2,3,0:T(8,128)} %collective-permute-done.16) | data formatting | bytes 44064 | tf_op jit(solution)/shard_map/ppermute | solution.py:22
  189.0 3.2 %copy.215 = f32[9,34,18,1]{3,2,1,0:T(8,128)} copy(f32[9,34,18,1]{1,2,3,0:T(8,128)S(1)} %collective-permute-done.17) | data formatting | bytes 44064 | tf_op jit(solution)/shard_map/ppermute | solution.py:20
  192.2 11.2 %pad_maximum_fusion.1 = (f32[9,34,18,129]{3,2,1,0:T(8,128)S(1)}, f32[9,34,18,129]{3,2,1,0:T(8,128)}) fusion(f32[9,34,18,1]{3,2,1,0:T(8,128)} %copy.212, f32[9,34,1,128]{3,2,1,0:T(1,128)S(1)} %copy.210, f32[9,1,16,128]{3,2,1,0:T(8,128)S(1)} %collective-permute-done.13, f32[9,32,16,128]{3,2,1,0:T(8,128)} %fusion.30, ...), kind=kLoop, calls=%fused_computation.2 | loop fusion | flops 7105320 | bytes 8548416 | tf_op jit(solution)/shard_map/concatenate | solution.py:18
  203.4 29.8 %multiply_reduce_fusion = (f32[9]{0:T(128)S(1)}, f32[9,32,16,128]{3,2,1,0:T(8,128)}) fusion(f32[32,16,128]{2,1,0:T(8,128)} %slice.847, f32[9,34,18,129]{3,2,1,0:T(8,128)} %get-tuple-element.15, f32[32,16,128]{2,1,0:T(8,128)} %get-tuple-element.62, f32[9,34,17,128]{3,2,1,0:T(8,128)} %get-tuple-element.21, f32[32,16,128]{2,1,0:T(8,128)} %get-tuple-element.63, ...), kind=kLoop, calls=%fused_computation.121 | loop fusion | flops 34209784 | bytes 69091360 | tf_op jit(solution)/shard_map/reduce_sum | solution.py:101
  233.2 43.0 %psum.7 = f32[9]{0:T(128)S(1)} all-reduce(f32[9]{0:T(128)S(1)} %get-tuple-element.4), channel_id=1, replica_groups=mesh['gx'=4,'gy'=4,'gz'=2] {'gx','gy','gz'}, use_global_device_ids=true, to_apply=%region_1.2 | all-reduce | flops 9 | bytes 72 | tf_op jit(solution)/shard_map/psum | solution.py:102
  (57 shorter events, 14.5 us)
Async XLA Ops:
  2.8 6.6 %collective-permute-start = (s32[3,2,16,128]{3,2,1,0:T(8,128)S(1)}, s32[3,2,16,128]{3,2,1,0:T(8,128)S(1)}, u32[]{:S(2)}, u32[]{:S(2)}) collective-permute-start(s32[3,2,16,128]{3,2,1,0:T(8,128)S(1)} %get-tuple-element.91), channel_id=1, source_target_pairs={{0,8},{8,16},{16,24},{1,9},{9,17},{17,25},{2,10},{10,18},{18,26},{... | collective-permute-start | bytes 147464 | tf_op jit(solution)/shard_map/ppermute | solution.py:20
  7.7 6.0 %collective-permute-start.1 = (s32[3,2,16,128]{3,2,1,0:T(8,128)S(1)}, s32[3,2,16,128]{3,2,1,0:T(8,128)S(1)}, u32[]{:S(2)}, u32[]{:S(2)}) collective-permute-start(s32[3,2,16,128]{3,2,1,0:T(8,128)S(1)} %get-tuple-element.92), channel_id=1, source_target_pairs={{8,0},{16,8},{24,16},{9,1},{17,9},{25,17},{10,2},{18,10},{26,18},{... | collective-permute-start | bytes 147464 | tf_op jit(solution)/shard_map/ppermute | solution.py:22
  9.4 14.5 %copy-start.5 = (s32[3,2,16,128]{3,2,1,0:T(8,128)}, s32[3,2,16,128]{3,2,1,0:T(8,128)S(1)}, u32[]{:S(2)}) copy-start(s32[3,2,16,128]{3,2,1,0:T(8,128)S(1)} %collective-permute-done) | copy-start | bytes 147460
  13.7 10.2 %copy-start.6 = (s32[3,2,16,128]{3,2,1,0:T(8,128)}, s32[3,2,16,128]{3,2,1,0:T(8,128)S(1)}, u32[]{:S(2)}) copy-start(s32[3,2,16,128]{3,2,1,0:T(8,128)S(1)} %collective-permute-done.1) | copy-start | bytes 147460
  13.8 5.8 %collective-permute-start.2 = (s32[3,36,2,128]{3,2,1,0:T(2,128)S(1)}, s32[3,36,2,128]{3,2,1,0:T(2,128)S(1)}, u32[]{:S(2)}, u32[]{:S(2)}) collective-permute-start(s32[3,36,2,128]{3,2,1,0:T(2,128)S(1)} %get-tuple-element.87), channel_id=1, source_target_pairs={{0,2},{2,4},{4,6},{1,3},{3,5},{5,7},{8,10},{10,12},{12,14},{9,11},... | collective-permute-start | bytes 331784 | tf_op jit(solution)/shard_map/ppermute | solution.py:20
  17.3 6.6 %collective-permute-start.3 = (s32[3,36,2,128]{3,2,1,0:T(2,128)S(1)}, s32[3,36,2,128]{3,2,1,0:T(2,128)S(1)}, u32[]{:S(2)}, u32[]{:S(2)}) collective-permute-start(s32[3,36,2,128]{3,2,1,0:T(2,128)S(1)} %get-tuple-element.88), channel_id=1, source_target_pairs={{2,0},{4,2},{6,4},{3,1},{5,3},{7,5},{10,8},{12,10},{14,12},{11,9},... | collective-permute-start | bytes 331784 | tf_op jit(solution)/shard_map/ppermute | solution.py:22
  23.9 0.6 copy-start.4
  26.3 3.1 %collective-permute-start.4 = (s32[3,36,20,2]{1,3,2,0:T(2,128)}, s32[3,36,20,2]{1,3,2,0:T(2,128)S(1)}, u32[]{:S(2)}, u32[]{:S(2)}) collective-permute-start(s32[3,36,20,2]{1,3,2,0:T(2,128)} %copy.193), channel_id=1, source_target_pairs={{0,1},{2,3},{4,5},{6,7},{8,9},{10,11},{12,13},{14,15},{16,17},{18,... | collective-permute-start | bytes 51848 | tf_op jit(solution)/shard_map/ppermute | solution.py:20
  28.2 3.3 %collective-permute-start.5 = (s32[3,36,20,2]{1,3,2,0:T(2,128)S(1)}, s32[3,36,20,2]{1,3,2,0:T(2,128)}, u32[]{:S(2)}, u32[]{:S(2)}) collective-permute-start(s32[3,36,20,2]{1,3,2,0:T(2,128)S(1)} %copy.194), channel_id=1, source_target_pairs={{1,0},{3,2},{5,4},{7,6},{9,8},{11,10},{13,12},{15,14},{17,16},{19,... | collective-permute-start | bytes 51848 | tf_op jit(solution)/shard_map/ppermute | solution.py:22
  37.2 3.5 %copy-start.2 = (f32[36,20,132]{2,1,0:T(8,128)}, f32[36,20,132]{2,1,0:T(8,128)S(1)}, u32[]{:S(2)}) copy-start(f32[36,20,132]{2,1,0:T(8,128)S(1)} %convert_multiply_fusion) | copy-start | bytes 1140484
  40.6 5.7 %copy-start.3 = (f32[9,32,16,128]{3,2,1,0:T(8,128)S(1)}, f32[9,32,16,128]{3,2,1,0:T(8,128)}, u32[]{:S(2)}) copy-start(f32[9,32,16,128]{3,2,1,0:T(8,128)} %param.5) | copy-start | bytes 7077892
  46.5 38.1 %copy-start.1 = (f32[9,32,16,128]{3,2,1,0:T(8,128)}, f32[9,32,16,128]{3,2,1,0:T(8,128)S(1)}, u32[]{:S(2)}) copy-start(f32[9,32,16,128]{3,2,1,0:T(8,128)S(1)} %broadcast_multiply_fusion) | copy-start | bytes 7077892
  46.6 11.0 %collective-permute-start.6 = (f32[9,1,16,128]{3,2,1,0:T(8,128)S(1)}, f32[9,1,16,128]{3,2,1,0:T(8,128)S(1)}, u32[]{:S(2)}, u32[]{:S(2)}) collective-permute-start(f32[9,1,16,128]{3,2,1,0:T(8,128)S(1)} %get-tuple-element.30), channel_id=1, source_target_pairs={{0,8},{8,16},{16,24},{1,9},{9,17},{17,25},{2,10},{10,18},{18,26},{... | collective-permute-start | bytes 221192 | tf_op jit(solution)/shard_map/ppermute | solution.py:20
  50.9 6.7 %collective-permute-start.7 = (f32[9,1,16,128]{3,2,1,0:T(8,128)S(1)}, f32[9,1,16,128]{3,2,1,0:T(8,128)S(1)}, u32[]{:S(2)}, u32[]{:S(2)}) collective-permute-start(f32[9,1,16,128]{3,2,1,0:T(8,128)S(1)} %get-tuple-element.31), channel_id=1, source_target_pairs={{8,0},{16,8},{24,16},{9,1},{17,9},{25,17},{10,2},{18,10},{26,18},{... | collective-permute-start | bytes 221192 | tf_op jit(solution)/shard_map/ppermute | solution.py:22
  57.9 9.1 %collective-permute-start.9 = (f32[9,34,1,128]{3,1,2,0:T(8,128)S(1)}, f32[9,34,1,128]{3,1,2,0:T(8,128)S(1)}, u32[]{:S(2)}, u32[]{:S(2)}) collective-permute-start(f32[9,34,1,128]{3,1,2,0:T(8,128)S(1)} %copy.198), channel_id=1, source_target_pairs={{2,0},{4,2},{6,4},{3,1},{5,3},{7,5},{10,8},{12,10},{14,12},{11,9},... | collective-permute-start | bytes 470024 | tf_op jit(solution)/shard_map/ppermute | solution.py:22
  59.2 8.5 %collective-permute-start.8 = (f32[9,34,1,128]{3,1,2,0:T(8,128)S(1)}, f32[9,34,1,128]{3,1,2,0:T(8,128)S(1)}, u32[]{:S(2)}, u32[]{:S(2)}) collective-permute-start(f32[9,34,1,128]{3,1,2,0:T(8,128)S(1)} %copy.197), channel_id=1, source_target_pairs={{0,2},{2,4},{4,6},{1,3},{3,5},{5,7},{8,10},{10,12},{12,14},{9,11},... | collective-permute-start | bytes 470024 | tf_op jit(solution)/shard_map/ppermute | solution.py:20
  79.7 12.6 %collective-permute-start.11 = (f32[9,34,18,1]{1,2,3,0:T(8,128)S(1)}, f32[9,34,18,1]{1,2,3,0:T(8,128)S(1)}, u32[]{:S(2)}, u32[]{:S(2)}) collective-permute-start(f32[9,34,18,1]{1,2,3,0:T(8,128)S(1)} %copy.204), channel_id=1, source_target_pairs={{1,0},{3,2},{5,4},{7,6},{9,8},{11,10},{13,12},{15,14},{17,16},{19,... | collective-permute-start | bytes 66104 | tf_op jit(solution)/shard_map/ppermute | solution.py:22
  81.0 7.4 %collective-permute-start.10 = (f32[9,34,18,1]{1,2,3,0:T(8,128)S(1)}, f32[9,34,18,1]{1,2,3,0:T(8,128)}, u32[]{:S(2)}, u32[]{:S(2)}) collective-permute-start(f32[9,34,18,1]{1,2,3,0:T(8,128)S(1)} %copy.201), channel_id=1, source_target_pairs={{0,1},{2,3},{4,5},{6,7},{8,9},{10,11},{12,13},{14,15},{16,17},{18,... | collective-permute-start | bytes 66104 | tf_op jit(solution)/shard_map/ppermute | solution.py:20
  144.3 22.1 %copy-start = (f32[9,32,16,128]{3,2,1,0:T(8,128)S(1)}, f32[9,32,16,128]{3,2,1,0:T(8,128)}, u32[]{:S(2)}) copy-start(f32[9,32,16,128]{3,2,1,0:T(8,128)} %fusion.30) | copy-start | bytes 7077892
  144.3 6.4 %collective-permute-start.12 = (f32[9,1,16,128]{3,2,1,0:T(8,128)S(1)}, f32[9,1,16,128]{3,2,1,0:T(8,128)S(1)}, u32[]{:S(2)}, u32[]{:S(2)}) collective-permute-start(f32[9,1,16,128]{3,2,1,0:T(8,128)S(1)} %get-tuple-element.28), channel_id=1, source_target_pairs={{0,8},{8,16},{16,24},{1,9},{9,17},{17,25},{2,10},{10,18},{18,26},{... | collective-permute-start | bytes 221192 | tf_op jit(solution)/shard_map/ppermute | solution.py:20
  148.7 6.2 %collective-permute-start.13 = (f32[9,1,16,128]{3,2,1,0:T(8,128)S(1)}, f32[9,1,16,128]{3,2,1,0:T(8,128)S(1)}, u32[]{:S(2)}, u32[]{:S(2)}) collective-permute-start(f32[9,1,16,128]{3,2,1,0:T(8,128)S(1)} %get-tuple-element.29), channel_id=1, source_target_pairs={{8,0},{16,8},{24,16},{9,1},{17,9},{25,17},{10,2},{18,10},{26,18},{... | collective-permute-start | bytes 221192 | tf_op jit(solution)/shard_map/ppermute | solution.py:22
  156.9 8.6 %collective-permute-start.15 = (f32[9,34,1,128]{3,1,2,0:T(8,128)S(1)}, f32[9,34,1,128]{3,1,2,0:T(8,128)S(1)}, u32[]{:S(2)}, u32[]{:S(2)}) collective-permute-start(f32[9,34,1,128]{3,1,2,0:T(8,128)S(1)} %copy.208), channel_id=1, source_target_pairs={{2,0},{4,2},{6,4},{3,1},{5,3},{7,5},{10,8},{12,10},{14,12},{11,9},... | collective-permute-start | bytes 470024 | tf_op jit(solution)/shard_map/ppermute | solution.py:22
  158.2 8.1 %collective-permute-start.14 = (f32[9,34,1,128]{3,1,2,0:T(8,128)S(1)}, f32[9,34,1,128]{3,1,2,0:T(8,128)S(1)}, u32[]{:S(2)}, u32[]{:S(2)}) collective-permute-start(f32[9,34,1,128]{3,1,2,0:T(8,128)S(1)} %copy.207), channel_id=1, source_target_pairs={{0,2},{2,4},{4,6},{1,3},{3,5},{5,7},{8,10},{10,12},{12,14},{9,11},... | collective-permute-start | bytes 470024 | tf_op jit(solution)/shard_map/ppermute | solution.py:20
  178.5 10.4 %collective-permute-start.17 = (f32[9,34,18,1]{1,2,3,0:T(8,128)S(1)}, f32[9,34,18,1]{1,2,3,0:T(8,128)S(1)}, u32[]{:S(2)}, u32[]{:S(2)}) collective-permute-start(f32[9,34,18,1]{1,2,3,0:T(8,128)S(1)} %copy.214), channel_id=1, source_target_pairs={{0,1},{2,3},{4,5},{6,7},{8,9},{10,11},{12,13},{14,15},{16,17},{18,... | collective-permute-start | bytes 66104 | tf_op jit(solution)/shard_map/ppermute | solution.py:20
  179.8 5.1 %collective-permute-start.16 = (f32[9,34,18,1]{1,2,3,0:T(8,128)S(1)}, f32[9,34,18,1]{1,2,3,0:T(8,128)}, u32[]{:S(2)}, u32[]{:S(2)}) collective-permute-start(f32[9,34,18,1]{1,2,3,0:T(8,128)S(1)} %copy.211), channel_id=1, source_target_pairs={{1,0},{3,2},{5,4},{7,6},{9,8},{11,10},{13,12},{15,14},{17,16},{19,... | collective-permute-start | bytes 66104 | tf_op jit(solution)/shard_map/ppermute | solution.py:22
where the time goes:
time: 278 us; the launch traced here: 277 us
  other arithmetic  124 us (45%)
  local copies, waits for them, and re-layouts  45.8 us (16%)
  starting transfers between devices  44.9 us (16%)
  blocking collectives  43 us (15%)
  waiting for transfers between devices  17.5 us (6%)
    psum x1, blocking collectives, per_device(): lax.psum(local_sums, ('gx', 'gy', 'gz')) / math.sqrt(cell_count)  43 us
    div x1, other arithmetic, per_device(): quotas = amounts / (gathered + beyond)  36.9 us
    concatenate x8, other arithmetic, padded(): jnp.concatenate([lax.ppermute(tail, axis, [(i, (i + 1) % count) for i in...  35.3 us
    ppermute x9, starting transfers between devices, padded(): lax.ppermute(tail, axis, [(i, (i + 1) % count) for i in range(ends)])  33.3 us
    reduce_sum x1, other arithmetic, per_device(): local_sums = jnp.sum(volume_mid[None] * redistributed, axis=(1, 2, 3))  29.8 us
    ppermute x9, waiting for transfers between devices, padded(): lax.ppermute(head, axis, [((i + 1) % count, i) for i in range(ends)])  14.2 us
    slice x9, local copies, waits for them, and re-layouts, padded(): lax.slice_in_dim(cells, cells.shape[dim] - width, cells.shape[dim], axis=...  13.8 us
    slice x6, local copies, waits for them, and re-layouts, padded(): head = lax.slice_in_dim(cells, 0, width, axis=dim)  12 us
  transfers between devices with their start and end apart: 18, of which 9 were waited for; matrix products, arithmetic and copies ran while one was open for 10% of the time, Pallas kernels for 0%

commit v1 on v0

v1 whole, which is shorter than its diff:
```python
import functools
import math

import jax
import jax.numpy as jnp
from jax import lax
from jax.experimental import pallas as pl
from jax.experimental.pallas import tpu as pltpu
from jax.sharding import PartitionSpec as P

CENTER = 8192
OFFSETS = [(a, b, c) for a in (-1, 0, 1) for b in (-1, 0, 1) for c in (-1, 0, 1)]
AXES = ("gx", "gy", "gz")
MESH = pl.DeviceIdType.MESH
LANES = 128
TILE = 8


def kernel(
    nx, ny, scale,
    prov, flag, code, vol, area,
    out, change,
    codes, codes_l, codes_r, carried, quotas, left, right, scaling,
    zs_i, zl_i, zr_i, zs_f, zl_f, zr_f, ys_i, yr_i, ys_f, yr_f, sums, peers,
    send, recv, peer_send, peer_recv,
):
    nspec = prov.shape[0]
    pitch = ny + TILE
    planes = nx + 2
    rows = TILE + planes * pitch
    tiles = ny // TILE
    here = {axis: lax.axis_index(axis) for axis in AXES}
    size = {axis: lax.axis_size(axis) for axis in AXES}
    lane = lax.broadcasted_iota(jnp.int32, (TILE, LANES), 1)

    barrier = pltpu.get_barrier_semaphore()
    for axis in AXES:
        for k in range(1, size[axis]):
            pl.semaphore_signal(
                barrier, inc=1, device_id={axis: lax.rem(here[axis] + k, size[axis])}, device_id_type=MESH
            )
    pl.semaphore_wait(barrier, sum(size[axis] - 1 for axis in AXES))

    def first(x):
        return TILE + x * pitch

    def own_tile(t):
        row = TILE + (t // tiles + 1) * pitch + lax.rem(t, tiles) * TILE
        return pl.multiple_of(row, TILE), pl.multiple_of(t * TILE, TILE)

    def links(axis, exchange, pairs):
        number = 2 * AXES.index(axis)
        n = size[axis]
        copies = []
        for way, (source, landing) in enumerate(pairs):
            step = 1 if way == 0 else n - 1
            copies.append(
                pltpu.make_async_remote_copy(
                    src_ref=source, dst_ref=landing,
                    send_sem=send.at[exchange, number + way], recv_sem=recv.at[exchange, number + way],
                    device_id={axis: lax.rem(here[axis] + step, n)}, device_id_type=MESH,
                )
            )
        return copies

    def has(axis):
        return here[axis] > 0, here[axis] < size[axis] - 1

    def start(axis, copies):
        below, above = has(axis)
        pl.when(above)(copies[0].start)
        pl.when(below)(copies[1].start)

    def finish(axis, copies):
        below, above = has(axis)
        pl.when(above)(copies[0].wait_send)
        pl.when(below)(copies[0].wait_recv)
        pl.when(below)(copies[1].wait_send)
        pl.when(above)(copies[1].wait_recv)

    def pack(packed, value, field):
        if packed is None:
            packed = jnp.zeros_like(value)
        keep = (lane == 2 * field) | (lane == (2 * field + LANES - 1) % LANES)
        rolled = value if field == 0 else pltpu.roll(value, 2 * field, 1)
        return jnp.where(keep, rolled, packed)

    def exchange(number, buf, zs, zl, zr, ys, yr, fields, between=None):
        zero = jnp.zeros((TILE, LANES), buf.dtype)
        z_copies = links("gz", number, ((zs, zl), (zs, zr)))
        start("gz", z_copies)
        finish("gz", z_copies)
        below, above = has("gz")
        odd = (lane & 1) == 1

        def place(t, carry):
            row, at = own_tile(t)
            low = jnp.where(below, zl[pl.ds(at, TILE), :], zero)
            high = jnp.where(above, zr[pl.ds(at, TILE), :], zero)
            buf[fields, pl.ds(row, TILE), :] = jnp.where(odd, low, high)
            return carry

        lax.fori_loop(0, nx * tiles, place, 0)
        x_copies = links(
            "gx", number,
            (
                (buf.at[:, pl.ds(first(nx), ny), :], buf.at[:, pl.ds(first(0), ny), :]),
                (buf.at[:, pl.ds(first(1), ny), :], buf.at[:, pl.ds(first(nx + 1), ny), :]),
            ),
        )
        start("gx", x_copies)
        if between is not None:
            between("gx")
        below, above = has("gx")

        def blank(x):
            for field in range(fields + 1):
                buf[field, pl.ds(first(x), ny), :] = jnp.zeros((ny, LANES), buf.dtype)

        pl.when(jnp.logical_not(below))(functools.partial(blank, 0))
        pl.when(jnp.logical_not(above))(functools.partial(blank, nx + 1))
        finish("gx", x_copies)

        chunks = [(x, min(TILE, planes - x)) for x in range(0, planes, TILE)]

        def gather(field, carry):
            for x, count in chunks:
                ys[0, field, pl.ds(x, count), :] = buf[field, pl.ds(first(x) + ny - 1, count, stride=pitch), :]
                ys[1, field, pl.ds(x, count), :] = buf[field, pl.ds(first(x), count, stride=pitch), :]
            return carry

        lax.fori_loop(0, fields + 1, gather, 0)
        y_copies = links("gy", number, ((ys.at[0], yr.at[0]), (ys.at[1], yr.at[1])))
        start("gy", y_copies)
        if between is not None:
            between("gy")
        finish("gy", y_copies)
        below, above = has("gy")

        def spread(field, carry):
            for x, count in chunks:
                blank_rows = jnp.zeros((count, LANES), buf.dtype)
                low = jnp.where(below, yr[0, field, pl.ds(x, count), :], blank_rows)
                high = jnp.where(above, yr[1, field, pl.ds(x, count), :], blank_rows)
                buf[field, pl.ds(first(x) - 1, count, stride=pitch), :] = low
                buf[field, pl.ds(first(x) + ny, count, stride=pitch), :] = high
            return carry

        lax.fori_loop(0, fields + 1, spread, 0)

    def shift(buf, to_left, to_right, fields):
        def body(t, carry):
            at = pl.ds(pl.multiple_of(t * TILE, TILE), TILE)
            ends = buf[fields, at, :]
            for field in range(fields):
                end = ends if field == 0 else pltpu.roll(ends, LANES - 2 * field, 1)
                value = buf[field, at, :]
                to_left[field, at, :] = pltpu.roll(jnp.where(lane == LANES - 1, end, value), 1, 1)
                to_right[field, at, :] = pltpu.roll(jnp.where(lane == 0, end, value), LANES - 1, 1)
            return carry

        lax.fori_loop(0, rows // TILE, body, 0)

    def fill(t, carry):
        row, at = own_tile(t)
        own = pl.ds(at, TILE)
        value = jnp.where(flag[own, :] == 1, code[own, :] | CENTER, CENTER)
        codes[0, pl.ds(row, TILE), :] = value
        zs_i[own, :] = pack(None, value, 0)
        return carry

    lax.fori_loop(0, nx * tiles, fill, 0)
    exchange(0, codes, zs_i, zl_i, zr_i, ys_i, yr_i, 1)
    shift(codes, codes_l, codes_r, 1)
    code_at = {-1: codes_l, 0: codes, 1: codes_r}

    sums[...] = jnp.zeros(sums.shape, jnp.float32)

    def weigh(t, carry):
        row, at = own_tile(t)
        own = pl.ds(at, TILE)
        counted = jnp.zeros((TILE, LANES), jnp.int32)
        for position, (a, b, c) in enumerate(OFFSETS):
            near = code_at[-c][0, pl.ds(row - a * pitch - b, TILE), :]
            counted = counted + (lax.shift_right_logical(near, position) & 1)
        is_cut = flag[own, :] == 1
        volume = jnp.where(is_cut, vol[own, :], 256).astype(jnp.float32) * (1.0 / 256.0)
        face = jnp.where(is_cut, area[own, :], 256).astype(jnp.float32) * (1.0 / 256.0)
        share = 1.0 / counted.astype(jnp.float32)
        scaling[own, :] = face * share
        weight = volume * share
        packed = None
        for s in range(nspec):
            p = prov[s, own, :]
            sums[s] = sums[s] + volume * p
            value = weight * p
            carried[s, pl.ds(row, TILE), :] = value
            packed = pack(packed, value, s)
        value = weight * face
        carried[nspec, pl.ds(row, TILE), :] = value
        zs_f[0, own, :] = pack(packed, value, nspec)
        return carry

    lax.fori_loop(0, nx * tiles, weigh, 0)

    def peer_copies(axis):
        n = size[axis]
        number = AXES.index(axis)
        return [
            pltpu.make_async_remote_copy(
                src_ref=peers.at[number, here[axis]], dst_ref=peers.at[number, here[axis]],
                send_sem=peer_send.at[number, k], recv_sem=peer_recv.at[number, k],
                device_id={axis: lax.rem(here[axis] + k, n)}, device_id_type=MESH,
            )
            for k in range(1, n)
        ]

    def total(axis):
        number = AXES.index(axis)
        value = peers[number, 0]
        for k in range(1, size[axis]):
            value = value + peers[number, k]
        return value

    def reduce_start(axis, value):
        peers[AXES.index(axis), here[axis]] = value
        for copy in peer_copies(axis):
            copy.start()

    def reduce_finish(axis):
        for copy in peer_copies(axis):
            copy.wait()
        return total(axis)

    local = jnp.concatenate(
        [jnp.sum(sums[s], axis=0, keepdims=True) for s in range(nspec)]
        + [jnp.zeros((peers.shape[2] - nspec, LANES), jnp.float32)],
        axis=0,
    )
    reduce_start("gx", local)

    def between(axis):
        if axis == "gx":
            reduce_start("gy", reduce_finish("gx"))
        else:
            reduce_start("gz", reduce_finish("gy"))

    exchange(1, carried, zs_f.at[0], zl_f.at[0], zr_f.at[0], ys_f.at[0], yr_f.at[0], nspec + 1, between)
    summed = reduce_finish("gz")
    change[...] = jnp.broadcast_to(jnp.sum(summed, axis=1, keepdims=True) * scale, change.shape)
    shift(carried, left, right, nspec + 1)
    carried_at = {-1: left, 0: carried, 1: right}

    def quota(t, carry):
        row, at = own_tile(t)
        mine = codes[0, pl.ds(row, TILE), :]
        zero = jnp.zeros((TILE, LANES), jnp.float32)
        totals = [zero] * (nspec + 1)
        for position, (a, b, c) in enumerate(OFFSETS):
            present = (mine & (1 << position)) != 0
            near = pl.ds(row + a * pitch + b, TILE)
            for s in range(nspec + 1):
                totals[s] = totals[s] + jnp.where(present, carried_at[c][s, near, :], zero)
        inverse = 1.0 / totals[nspec]
        packed = None
        for s in range(nspec):
            value = totals[s] * inverse
            quotas[s, pl.ds(row, TILE), :] = value
            packed = pack(packed, value, s)
        zs_f[1, pl.ds(at, TILE), :] = packed
        return carry

    lax.fori_loop(0, nx * tiles, quota, 0)
    exchange(
        2, quotas, zs_f.at[1], zl_f.at[1], zr_f.at[1],
        ys_f.at[1, :, pl.ds(0, nspec + 1)], yr_f.at[1, :, pl.ds(0, nspec + 1)], nspec,
    )
    shift(quotas, left, right, nspec)
    quotas_at = {-1: left, 0: quotas, 1: right}

    def scatter(t, carry):
        row, at = own_tile(t)
        own = pl.ds(at, TILE)
        zero = jnp.zeros((TILE, LANES), jnp.float32)
        totals = [zero] * nspec
        for position, (a, b, c) in enumerate(OFFSETS):
            near = pl.ds(row - a * pitch - b, TILE)
            present = (code_at[-c][0, near, :] & (1 << position)) != 0
            for s in range(nspec):
                totals[s] = totals[s] + jnp.where(present, quotas_at[-c][s, near, :], zero)
        factor = scaling[own, :]
        for s in range(nspec):
            out[s, own, :] = factor * totals[s]
        return carry

    lax.fori_loop(0, nx * tiles, scatter, 0)


def per_device(provisional, cut_flag, cut_code, volume_level, area_level):
    nspec, nx, ny, nz = provisional.shape
    assert nz == LANES and ny % TILE == 0
    own = nx * ny
    planes = nx + 2
    rows = TILE + planes * (ny + TILE)
    slab = -(-planes // TILE) * TILE
    most = max(lax.axis_size(axis) for axis in AXES)
    cells = own * nz * math.prod(lax.axis_size(axis) for axis in AXES)
    high = -(-nspec // TILE) * TILE
    f32, i32 = jnp.float32, jnp.int32
    vmem = pl.BlockSpec(memory_space=pltpu.VMEM)
    shapes = [
        ((2, rows, nz), i32), ((1, rows, nz), i32), ((1, rows, nz), i32),
        ((nspec + 2, rows, nz), f32), ((nspec + 1, rows, nz), f32),
        ((nspec + 1, rows, nz), f32), ((nspec + 1, rows, nz), f32),
        ((own, nz), f32),
        ((own, nz), i32), ((own, nz), i32), ((own, nz), i32),
        ((2, own, nz), f32), ((2, own, nz), f32), ((2, own, nz), f32),
        ((2, 2, slab, nz), i32), ((2, 2, slab, nz), i32),
        ((2, 2, nspec + 2, slab, nz), f32), ((2, 2, nspec + 2, slab, nz), f32),
        ((nspec, TILE, nz), f32), ((3, most, high, nz), f32),
    ]
    out, change = pl.pallas_call(
        functools.partial(kernel, nx, ny, 1.0 / math.sqrt(cells)),
        out_shape=(
            jax.ShapeDtypeStruct((nspec, own, nz), f32),
            jax.ShapeDtypeStruct((high, nz), f32),
        ),
        in_specs=[vmem] * 5,
        out_specs=(vmem, vmem),
        scratch_shapes=[pltpu.VMEM(shape, kind) for shape, kind in shapes]
        + [
            pltpu.SemaphoreType.DMA((3, 6)), pltpu.SemaphoreType.DMA((3, 6)),
            pltpu.SemaphoreType.DMA((3, most)), pltpu.SemaphoreType.DMA((3, most)),
        ],
        compiler_params=pltpu.CompilerParams(
            collective_id=0, has_side_effects=True, vmem_limit_bytes=60 * 1024 * 1024
        ),
    )(
        provisional.reshape(nspec, own, nz),
        cut_flag.reshape(own, nz),
        cut_code.reshape(own, nz),
        volume_level.reshape(own, nz),
        area_level.reshape(own, nz),
    )
    return out.reshape(provisional.shape), change[:nspec, 0]


def solution(mesh):
    spec = P("gx", "gy", "gz")
    wide = P(None, "gx", "gy", "gz")
    return jax.shard_map(
        per_device, mesh=mesh, in_specs=(wide, spec, spec, spec, spec), out_specs=(wide, P()), check_vma=False
    )
```

time: 278 us -> 120 us (0.43)
  other arithmetic: 124 us -> 0 us
  Pallas kernels: 0 us -> 114 us
  starting transfers between devices: 44.9 us -> 0 us
  blocking collectives: 43 us -> 0 us
  local copies, waits for them, and re-layouts: 45.8 us -> 4.54 us
  waiting for transfers between devices: 17.5 us -> 0 us
    pallas_call x0 -> x1, Pallas kernels: none -> 114 us  [per_device(): pl.pallas_call(functools.partial(kernel, nx, ny, 1.0 / math.sqrt(cells)),...]
    ppermute x18 -> x0, starting transfers between devices: 44.9 us -> none  [the longest x9 33.3 us: padded(): lax.ppermute(tail, axis, [(i, (i + 1) % count) for i in range(ends)])]
    div x6 -> x0, other arithmetic: 43.3 us -> none  [the longest x1 36.9 us: per_device(): quotas = amounts / (gathered + beyond)]
    psum x1 -> x0, blocking collectives: 43 us -> none  [per_device(): lax.psum(local_sums, ('gx', 'gy', 'gz')) / math.sqrt(cell_count)]
    concatenate x8 -> x0, other arithmetic: 35.3 us -> none  [padded(): jnp.concatenate([lax.ppermute(tail, axis, [(i, (i + 1) % count) for i in...]
    reduce_sum x1 -> x0, other arithmetic: 29.8 us -> none  [per_device(): local_sums = jnp.sum(volume_mid[None] * redistributed, axis=(1, 2, 3))]
    slice x17 -> x1, local copies, waits for them, and re-layouts: 28.1 us -> 1.32 us  [per_device(): return (out.reshape(provisional.shape), change[:nspec, 0])]
    ppermute x18 -> x0, waiting for transfers between devices: 17.5 us -> none  [the longest x9 14.2 us: padded(): lax.ppermute(head, axis, [((i + 1) % count, i) for i in range(ends)])]
  transfers between devices with their start and end apart: 18 -> 0, of which waited for: 9 -> 0; matrix products, arithmetic and copies ran while one was open for 10% -> 0% of each run, Pallas kernels for 0% -> 0%
where the time goes in v1:
time: 120 us
  Pallas kernels  114 us (95%)
  local copies, waits for them, and re-layouts  4.54 us (4%)
    pallas_call x1, Pallas kernels, per_device(): pl.pallas_call(functools.partial(kernel, nx, ny, 1.0 / math.sqrt(cells)),...  114 us
    unnamed x1, local copies, waits for them, and re-layouts  3.22 us

profile of v1, /device:TPU:0, one launch (start us, length us, event | category | flops | bytes accessed | tf_op | source)
XLA Modules:
  0.0 119.6 jit_solution(12298089330493342433)
XLA Ops:
  0.6 114.4 %shard_map.68 = (f32[9,512,128]{2,1,0:T(8,128)}, f32[16,128]{1,0:T(8,128)}) custom-call(f32[9,512,128]{2,1,0:T(8,128)} %bitcast.7, s32[512,128]{1,0:T(8,128)} %bitcast.8, s32[512,128]{1,0:T(8,128)} %bitcast.9, s32[512,128]{1,0:T(8,128)} %bitcast.10, s32[512,128]{1,0:T(8,128)} %bitcast.11), custom_call_target="tpu_custom_call" | custom-call | tf_op jit(solution)/shard_map/pallas_call | solution.py:322
  115.1 1.3 %slice_reduce_fusion = f32[9]{0:T(128)} fusion(f32[16,128]{1,0:T(8,128)} %get-tuple-element.5), kind=kLoop, calls=%fused_computation | loop fusion | bytes 72 | tf_op jit(solution)/shard_map/slice | solution.py:345
  116.4 3.2 %copy.8 = f32[9,32,16,128]{3,2,1,0:T(8,128)} copy(f32[9,32,16,128]{3,2,1,0:T(8,128)} %bitcast.6) | data formatting | bytes 4718592

commit v2 on v1

v2 whole, which is shorter than its diff:
```python
import functools
import math

import jax
import jax.numpy as jnp
from jax import lax
from jax.experimental import pallas as pl
from jax.experimental.pallas import tpu as pltpu
from jax.sharding import PartitionSpec as P

CENTER = 8192
OFFSETS = [(a, b, c) for a in (-1, 0, 1) for b in (-1, 0, 1) for c in (-1, 0, 1)]
AXES = ("gx", "gy", "gz")
MESH = pl.DeviceIdType.MESH
LANES = 128
TILE = 8
GROUP = 4


def kernel(
    nx, ny, scale,
    prov, flag, code, vol, area,
    out, change,
    codes, codes_l, codes_r, carried_a, carried_b, quotas_a, quotas_b, left_a, right_a, left_b, right_b,
    scaling, weights, inverse,
    zs_i, zl_i, zr_i, zs_f, zl_f, zr_f, ys_i, yr_i, ys_f, yr_f, sums, peers,
    send, recv, peer_send, peer_recv,
):
    nspec = prov.shape[0]
    pitch = ny + TILE
    planes = nx + 2
    rows = codes.shape[1]
    tiles = ny // TILE
    here = {axis: lax.axis_index(axis) for axis in AXES}
    size = {axis: lax.axis_size(axis) for axis in AXES}
    lane = lax.broadcasted_iota(jnp.int32, (TILE, LANES), 1)

    barrier = pltpu.get_barrier_semaphore()
    for axis in AXES:
        for k in range(1, size[axis]):
            pl.semaphore_signal(
                barrier, inc=1, device_id={axis: lax.rem(here[axis] + k, size[axis])}, device_id_type=MESH
            )
    pl.semaphore_wait(barrier, sum(size[axis] - 1 for axis in AXES))

    def first(x):
        return TILE + x * pitch

    def own_tile(t):
        row = TILE + (t // tiles + 1) * pitch + lax.rem(t, tiles) * TILE
        return pl.multiple_of(row, TILE), pl.multiple_of(t * TILE, TILE)

    def links(axis, exchange, pairs):
        number = 2 * AXES.index(axis)
        n = size[axis]
        copies = []
        for way, (source, landing) in enumerate(pairs):
            step = 1 if way == 0 else n - 1
            copies.append(
                pltpu.make_async_remote_copy(
                    src_ref=source, dst_ref=landing,
                    send_sem=send.at[exchange, number + way], recv_sem=recv.at[exchange, number + way],
                    device_id={axis: lax.rem(here[axis] + step, n)}, device_id_type=MESH,
                )
            )
        return copies

    def has(axis):
        return here[axis] > 0, here[axis] < size[axis] - 1

    def start(axis, copies):
        below, above = has(axis)
        pl.when(above)(copies[0].start)
        pl.when(below)(copies[1].start)

    def finish(axis, copies):
        below, above = has(axis)
        pl.when(above)(copies[0].wait_send)
        pl.when(below)(copies[0].wait_recv)
        pl.when(below)(copies[1].wait_send)
        pl.when(above)(copies[1].wait_recv)

    def pack(packed, value, field):
        if packed is None:
            packed = jnp.zeros_like(value)
        keep = (lane == 2 * field) | (lane == (2 * field + LANES - 1) % LANES)
        rolled = value if field == 0 else pltpu.roll(value, 2 * field, 1)
        return jnp.where(keep, rolled, packed)

    def exchange(number, buf, zs, zl, zr, ys, yr, fields):
        zero = jnp.zeros((TILE, LANES), buf.dtype)
        z_copies = links("gz", number, ((zs, zl), (zs, zr)))
        start("gz", z_copies)
        yield
        finish("gz", z_copies)
        below, above = has("gz")
        odd = (lane & 1) == 1

        def place(t, carry):
            row, at = own_tile(t)
            low = jnp.where(below, zl[pl.ds(at, TILE), :], zero)
            high = jnp.where(above, zr[pl.ds(at, TILE), :], zero)
            buf[fields, pl.ds(row, TILE), :] = jnp.where(odd, low, high)
            return carry

        lax.fori_loop(0, nx * tiles, place, 0, unroll=4)
        x_copies = links(
            "gx", number,
            (
                (buf.at[:, pl.ds(first(nx), ny), :], buf.at[:, pl.ds(first(0), ny), :]),
                (buf.at[:, pl.ds(first(1), ny), :], buf.at[:, pl.ds(first(nx + 1), ny), :]),
            ),
        )
        start("gx", x_copies)
        yield
        below, above = has("gx")

        def blank(x):
            for field in range(fields + 1):
                buf[field, pl.ds(first(x), ny), :] = jnp.zeros((ny, LANES), buf.dtype)

        pl.when(jnp.logical_not(below))(functools.partial(blank, 0))
        pl.when(jnp.logical_not(above))(functools.partial(blank, nx + 1))
        finish("gx", x_copies)

        chunks = [(x, min(TILE, planes - x)) for x in range(0, planes, TILE)]

        def gather(field, carry):
            for x, count in chunks:
                ys[0, field, pl.ds(x, count), :] = buf[field, pl.ds(first(x) + ny - 1, count, stride=pitch), :]
                ys[1, field, pl.ds(x, count), :] = buf[field, pl.ds(first(x), count, stride=pitch), :]
            return carry

        lax.fori_loop(0, fields + 1, gather, 0)
        y_copies = links("gy", number, ((ys.at[0], yr.at[0]), (ys.at[1], yr.at[1])))
        start("gy", y_copies)
        yield
        finish("gy", y_copies)
        below, above = has("gy")

        def spread(field, carry):
            for x, count in chunks:
                blank_rows = jnp.zeros((count, LANES), buf.dtype)
                low = jnp.where(below, yr[0, field, pl.ds(x, count), :], blank_rows)
                high = jnp.where(above, yr[1, field, pl.ds(x, count), :], blank_rows)
                buf[field, pl.ds(first(x) - 1, count, stride=pitch), :] = low
                buf[field, pl.ds(first(x) + ny, count, stride=pitch), :] = high
            return carry

        lax.fori_loop(0, fields + 1, spread, 0)
        yield

    def shift(buf, to_left, to_right, fields):
        def body(g, carry):
            at = [pl.ds(pl.multiple_of((g * GROUP + k) * TILE, TILE), TILE) for k in range(GROUP)]
            ends = [buf[fields, near, :] for near in at]
            for field in range(fields):
                end = [e if field == 0 else pltpu.roll(e, LANES - 2 * field, 1) for e in ends]
                for near, e in zip(at, end):
                    value = buf[field, near, :]
                    to_left[field, near, :] = pltpu.roll(jnp.where(lane == LANES - 1, e, value), 1, 1)
                    to_right[field, near, :] = pltpu.roll(jnp.where(lane == 0, e, value), LANES - 1, 1)
            return carry

        lax.fori_loop(0, rows // (GROUP * TILE), body, 0)

    def fill(t, carry):
        row, at = own_tile(t)
        own = pl.ds(at, TILE)
        value = jnp.where(flag[own, :] == 1, code[own, :] | CENTER, CENTER)
        codes[0, pl.ds(row, TILE), :] = value
        zs_i[own, :] = pack(None, value, 0)
        return carry

    count = nx * tiles

    def loop(body, part=0, parts=1, unroll=2):
        low, high = (count * k // (4 * parts) * 4 for k in (part, part + 1))
        if part == parts - 1:
            high = count
        lax.fori_loop(low, high, body, 0, unroll=unroll)

    cut = nspec // 2
    group_a, group_b = list(range(cut)), list(range(cut, nspec))

    def fractions(own):
        is_cut = flag[own, :] == 1
        volume = jnp.where(is_cut, vol[own, :], 256).astype(jnp.float32) * (1.0 / 256.0)
        face = jnp.where(is_cut, area[own, :], 256).astype(jnp.float32) * (1.0 / 256.0)
        return volume, face

    def peer_copies(axis):
        n = size[axis]
        number = AXES.index(axis)
        return [
            pltpu.make_async_remote_copy(
                src_ref=peers.at[number, here[axis]], dst_ref=peers.at[number, here[axis]],
                send_sem=peer_send.at[number, k], recv_sem=peer_recv.at[number, k],
                device_id={axis: lax.rem(here[axis] + k, n)}, device_id_type=MESH,
            )
            for k in range(1, n)
        ]

    def reduce_start(axis, value):
        peers[AXES.index(axis), here[axis]] = value
        for copy in peer_copies(axis):
            copy.start()

    def reduce_finish(axis):
        number = AXES.index(axis)
        for copy in peer_copies(axis):
            copy.wait()
        value = peers[number, 0]
        for k in range(1, size[axis]):
            value = value + peers[number, k]
        return value

    loop(fill, unroll=4)
    code_steps = exchange(0, codes, zs_i, zl_i, zr_i, ys_i, yr_i, 1)
    next(code_steps)
    sums[...] = jnp.zeros(sums.shape, jnp.float32)

    def add_up(t, totals):
        _, at = own_tile(t)
        own = pl.ds(at, TILE)
        volume, _ = fractions(own)
        return tuple(totals[s] + volume * prov[s, own, :] for s in range(nspec))

    totals = lax.fori_loop(0, count, add_up, tuple(jnp.zeros((TILE, LANES), jnp.float32) for _ in range(nspec)))
    for s in range(nspec):
        sums[s] = totals[s]
    next(code_steps)
    local = jnp.concatenate(
        [jnp.sum(sums[s], axis=0, keepdims=True) for s in range(nspec)]
        + [jnp.zeros((peers.shape[2] - nspec, LANES), jnp.float32)],
        axis=0,
    )
    reduce_start("gx", local)
    next(code_steps)
    next(code_steps)
    shift(codes, codes_l, codes_r, 1)
    code_at = {-1: codes_l, 0: codes, 1: codes_r}

    def weigh_a(t, carry):
        row, at = own_tile(t)
        own = pl.ds(at, TILE)
        counted = jnp.zeros((TILE, LANES), jnp.int32)
        for position, (a, b, c) in enumerate(OFFSETS):
            near = code_at[-c][0, pl.ds(row - a * pitch - b, TILE), :]
            counted = counted + (lax.shift_right_logical(near, position) & 1)
        volume, face = fractions(own)
        share = 1.0 / counted.astype(jnp.float32)
        scaling[own, :] = face * share
        weight = volume * share
        weights[own, :] = weight
        packed = None
        for f, s in enumerate(group_a):
            value = weight * prov[s, own, :]
            carried_a[f, pl.ds(row, TILE), :] = value
            packed = pack(packed, value, f)
        value = weight * face
        carried_a[cut, pl.ds(row, TILE), :] = value
        zs_f[0, own, :] = pack(packed, value, cut)
        return carry

    def weigh_b(t, carry):
        row, at = own_tile(t)
        own = pl.ds(at, TILE)
        weight = weights[own, :]
        packed = None
        for f, s in enumerate(group_b):
            value = weight * prov[s, own, :]
            carried_b[f, pl.ds(row, TILE), :] = value
            packed = pack(packed, value, f)
        zs_f[1, own, :] = packed
        return carry

    def exchange_f(number, buf, fields):
        k = number - 1
        return exchange(
            number, buf, zs_f.at[k], zl_f.at[k], zr_f.at[k],
            ys_f.at[k, :, pl.ds(0, fields + 1)], yr_f.at[k, :, pl.ds(0, fields + 1)], fields,
        )

    def taps(t, fields, at_shift, sign):
        row, _ = own_tile(t)
        zero = jnp.zeros((TILE, LANES), jnp.float32)
        found = [zero] * fields
        mine = codes[0, pl.ds(row, TILE), :] if sign > 0 else None
        for position, (a, b, c) in enumerate(OFFSETS):
            near = pl.ds(row + sign * (a * pitch + b), TILE)
            code_here = mine if sign > 0 else code_at[-c][0, near, :]
            present = (code_here & (1 << position)) != 0
            for f in range(fields):
                found[f] = found[f] + jnp.where(present, at_shift[sign * c][f, near, :], zero)
        return found

    def quota_a(t, carry):
        row, at = own_tile(t)
        found = taps(t, cut + 1, {-1: left_a, 0: carried_a, 1: right_a}, 1)
        inverted = 1.0 / found[cut]
        inverse[pl.ds(at, TILE), :] = inverted
        packed = None
        for f in range(cut):
            value = found[f] * inverted
            quotas_a[f, pl.ds(row, TILE), :] = value
            packed = pack(packed, value, f)
        zs_f[2, pl.ds(at, TILE), :] = packed
        return carry

    def quota_b(t, carry):
        row, at = own_tile(t)
        found = taps(t, len(group_b), {-1: left_b, 0: carried_b, 1: right_b}, 1)
        inverted = inverse[pl.ds(at, TILE), :]
        packed = None
        for f in range(len(group_b)):
            value = found[f] * inverted
            quotas_b[f, pl.ds(row, TILE), :] = value
            packed = pack(packed, value, f)
        zs_f[3, pl.ds(at, TILE), :] = packed
        return carry

    def scatter(group, buf, left, right, t, carry):
        _, at = own_tile(t)
        own = pl.ds(at, TILE)
        found = taps(t, len(group), {-1: left, 0: buf, 1: right}, -1)
        factor = scaling[own, :]
        for f, s in enumerate(group):
            out[s, own, :] = factor * found[f]
        return carry

    scatter_a = functools.partial(scatter, group_a, quotas_a, left_a, right_a)
    scatter_b = functools.partial(scatter, group_b, quotas_b, left_b, right_b)

    loop(weigh_a)
    steps_a = exchange_f(1, carried_a, cut + 1)
    next(steps_a)
    loop(weigh_b)
    steps_b = exchange_f(2, carried_b, len(group_b))
    next(steps_b)
    next(steps_a)
    next(steps_b)
    reduce_start("gy", reduce_finish("gx"))
    next(steps_a)
    next(steps_b)
    next(steps_a)
    shift(carried_a, left_a, right_a, cut + 1)
    loop(quota_a)
    steps_qa = exchange_f(3, quotas_a, cut)
    next(steps_qa)
    next(steps_b)
    shift(carried_b, left_b, right_b, len(group_b))
    next(steps_qa)
    loop(quota_b, 0, 2)
    next(steps_qa)
    loop(quota_b, 1, 2)
    steps_qb = exchange_f(4, quotas_b, len(group_b))
    next(steps_qb)
    reduce_start("gz", reduce_finish("gy"))
    next(steps_qa)
    next(steps_qb)
    shift(quotas_a, left_a, right_a, cut)
    next(steps_qb)
    loop(scatter_a)
    summed = reduce_finish("gz")
    change[...] = jnp.broadcast_to(jnp.sum(summed, axis=1, keepdims=True) * scale, change.shape)
    next(steps_qb)
    shift(quotas_b, left_b, right_b, len(group_b))
    loop(scatter_b)


def per_device(provisional, cut_flag, cut_code, volume_level, area_level):
    nspec, nx, ny, nz = provisional.shape
    assert nz == LANES and ny % TILE == 0
    own = nx * ny
    planes = nx + 2
    rows = -(-(TILE + planes * (ny + TILE)) // (GROUP * TILE)) * (GROUP * TILE)
    slab = -(-planes // TILE) * TILE
    most = max(lax.axis_size(axis) for axis in AXES)
    cells = own * nz * math.prod(lax.axis_size(axis) for axis in AXES)
    high = -(-nspec // TILE) * TILE
    cut = nspec // 2
    rest = nspec - cut
    f32, i32 = jnp.float32, jnp.int32
    vmem = pl.BlockSpec(memory_space=pltpu.VMEM)
    shapes = [
        ((2, rows, nz), i32), ((1, rows, nz), i32), ((1, rows, nz), i32),
        ((cut + 2, rows, nz), f32), ((rest + 1, rows, nz), f32),
        ((cut + 1, rows, nz), f32), ((rest + 1, rows, nz), f32),
        ((cut + 1, rows, nz), f32), ((cut + 1, rows, nz), f32),
        ((rest, rows, nz), f32), ((rest, rows, nz), f32),
        ((own, nz), f32), ((own, nz), f32), ((own, nz), f32),
        ((own, nz), i32), ((own, nz), i32), ((own, nz), i32),
        ((4, own, nz), f32), ((4, own, nz), f32), ((4, own, nz), f32),
        ((2, 2, slab, nz), i32), ((2, 2, slab, nz), i32),
        ((4, 2, rest + 1, slab, nz), f32), ((4, 2, rest + 1, slab, nz), f32),
        ((nspec, TILE, nz), f32), ((3, most, high, nz), f32),
    ]
    out, change = pl.pallas_call(
        functools.partial(kernel, nx, ny, 1.0 / math.sqrt(cells)),
        out_shape=(
            jax.ShapeDtypeStruct((nspec, own, nz), f32),
            jax.ShapeDtypeStruct((high, nz), f32),
        ),
        in_specs=[vmem] * 5,
        out_specs=(vmem, vmem),
        scratch_shapes=[pltpu.VMEM(shape, kind) for shape, kind in shapes]
        + [
            pltpu.SemaphoreType.DMA((5, 6)), pltpu.SemaphoreType.DMA((5, 6)),
            pltpu.SemaphoreType.DMA((3, most)), pltpu.SemaphoreType.DMA((3, most)),
        ],
        compiler_params=pltpu.CompilerParams(
            collective_id=0, has_side_effects=True, vmem_limit_bytes=60 * 1024 * 1024
        ),
    )(
        provisional.reshape(nspec, own, nz),
        cut_flag.reshape(own, nz),
        cut_code.reshape(own, nz),
        volume_level.reshape(own, nz),
        area_level.reshape(own, nz),
    )
    return out.reshape(provisional.shape), change[:nspec, 0]


def solution(mesh):
    spec = P("gx", "gy", "gz")
    wide = P(None, "gx", "gy", "gz")
    return jax.shard_map(
        per_device, mesh=mesh, in_specs=(wide, spec, spec, spec, spec), out_specs=(wide, P()), check_vma=False
    )
```

time: 120 us -> 81.9 us (0.68)
  Pallas kernels: 114 us -> 76.5 us
    pallas_call x1, Pallas kernels: 114 us -> 76.5 us  [per_device(): pl.pallas_call(functools.partial(kernel, nx, ny, 1.0 / math.sqrt(cells)),...]
where the time goes in v2:
time: 81.9 us; the launch traced here: 81.7 us
  Pallas kernels  76.5 us (93%)
  local copies, waits for them, and re-layouts  4.54 us (6%)
    pallas_call x1, Pallas kernels, per_device(): pl.pallas_call(functools.partial(kernel, nx, ny, 1.0 / math.sqrt(cells)),...  76.5 us
    unnamed x1, local copies, waits for them, and re-layouts  3.22 us

profile of v2, /device:TPU:0, one launch (start us, length us, event | category | flops | bytes accessed | tf_op | source)
XLA Modules:
  0.0 81.7 jit_solution(8067275884561000850)
XLA Ops:
  0.6 76.5 %shard_map.68 = (f32[9,512,128]{2,1,0:T(8,128)}, f32[16,128]{1,0:T(8,128)}) custom-call(f32[9,512,128]{2,1,0:T(8,128)} %bitcast.7, s32[512,128]{1,0:T(8,128)} %bitcast.8, s32[512,128]{1,0:T(8,128)} %bitcast.9, s32[512,128]{1,0:T(8,128)} %bitcast.10, s32[512,128]{1,0:T(8,128)} %bitcast.11), custom_call_target="tpu_custom_call" | custom-call | tf_op jit(solution)/shard_map/pallas_call | solution.py:399
  77.2 1.3 %slice_reduce_fusion = f32[9]{0:T(128)} fusion(f32[16,128]{1,0:T(8,128)} %get-tuple-element.5), kind=kLoop, calls=%fused_computation | loop fusion | bytes 72 | tf_op jit(solution)/shard_map/slice | solution.py:422
  78.5 3.2 %copy.8 = f32[9,32,16,128]{3,2,1,0:T(8,128)} copy(f32[9,32,16,128]{3,2,1,0:T(8,128)} %bitcast.6) | data formatting | bytes 4718592

commit v3 on v2

--- a/solution.py
+++ b/solution.py
@@ -14,7 +14,7 @@
 MESH = pl.DeviceIdType.MESH
 LANES = 128
 TILE = 8
-GROUP = 4
+GROUP = 16
 
 
 def kernel(
@@ -23,7 +23,7 @@
     out, change,
     codes, codes_l, codes_r, carried_a, carried_b, quotas_a, quotas_b, left_a, right_a, left_b, right_b,
     scaling, weights, inverse,
-    zs_i, zl_i, zr_i, zs_f, zl_f, zr_f, ys_i, yr_i, ys_f, yr_f, sums, peers,
+    zs_i, zl_i, zr_i, zs_f, zl_f, zr_f, ys_i, yr_i, ys_f, yr_f, peers,
     send, recv, peer_send, peer_recv,
 ):
     nspec = prov.shape[0]
@@ -155,11 +155,11 @@
             at = [pl.ds(pl.multiple_of((g * GROUP + k) * TILE, TILE), TILE) for k in range(GROUP)]
             ends = [buf[fields, near, :] for near in at]
             for field in range(fields):
-                end = [e if field == 0 else pltpu.roll(e, LANES - 2 * field, 1) for e in ends]
+                end = [(pltpu.roll(e, (LANES + 1 - 2 * field) % LANES, 1), pltpu.roll(e, (2 * LANES - 1 - 2 * field) % LANES, 1)) for e in ends]
                 for near, e in zip(at, end):
                     value = buf[field, near, :]
-                    to_left[field, near, :] = pltpu.roll(jnp.where(lane == LANES - 1, e, value), 1, 1)
-                    to_right[field, near, :] = pltpu.roll(jnp.where(lane == 0, e, value), LANES - 1, 1)
+                    to_left[field, near, :] = jnp.where(lane == 0, e[0], pltpu.roll(value, 1, 1))
+                    to_right[field, near, :] = jnp.where(lane == LANES - 1, e[1], pltpu.roll(value, LANES - 1, 1))
             return carry
 
         lax.fori_loop(0, rows // (GROUP * TILE), body, 0)
@@ -174,7 +174,7 @@
 
     count = nx * tiles
 
-    def loop(body, part=0, parts=1, unroll=2):
+    def loop(body, part=0, parts=1, unroll=4):
         low, high = (count * k // (4 * parts) * 4 for k in (part, part + 1))
         if part == parts - 1:
             high = count
@@ -218,7 +218,6 @@
     loop(fill, unroll=4)
     code_steps = exchange(0, codes, zs_i, zl_i, zr_i, ys_i, yr_i, 1)
     next(code_steps)
-    sums[...] = jnp.zeros(sums.shape, jnp.float32)
 
     def add_up(t, totals):
         _, at = own_tile(t)
@@ -226,18 +225,20 @@
         volume, _ = fractions(own)
         return tuple(totals[s] + volume * prov[s, own, :] for s in range(nspec))
 
-    totals = lax.fori_loop(0, count, add_up, tuple(jnp.zeros((TILE, LANES), jnp.float32) for _ in range(nspec)))
-    for s in range(nspec):
-        sums[s] = totals[s]
-    next(code_steps)
+    def add_part(part, totals):
+        low, high = (count * k // 12 * 4 for k in (part, part + 1))
+        return lax.fori_loop(low, high if part < 2 else count, add_up, totals, unroll=4)
+
+    totals = tuple(jnp.zeros((TILE, LANES), jnp.float32) for _ in range(nspec))
+    for part in range(3):
+        totals = add_part(part, totals)
+        next(code_steps)
     local = jnp.concatenate(
-        [jnp.sum(sums[s], axis=0, keepdims=True) for s in range(nspec)]
+        [jnp.sum(total, axis=0, keepdims=True) for total in totals]
         + [jnp.zeros((peers.shape[2] - nspec, LANES), jnp.float32)],
         axis=0,
     )
     reduce_start("gx", local)
-    next(code_steps)
-    next(code_steps)
     shift(codes, codes_l, codes_r, 1)
     code_at = {-1: codes_l, 0: codes, 1: codes_r}
 
@@ -394,7 +395,7 @@
         ((4, own, nz), f32), ((4, own, nz), f32), ((4, own, nz), f32),
         ((2, 2, slab, nz), i32), ((2, 2, slab, nz), i32),
         ((4, 2, rest + 1, slab, nz), f32), ((4, 2, rest + 1, slab, nz), f32),
-        ((nspec, TILE, nz), f32), ((3, most, high, nz), f32),
+        ((3, most, high, nz), f32),
     ]
     out, change = pl.pallas_call(
         functools.partial(kernel, nx, ny, 1.0 / math.sqrt(cells)),

time: 81.9 us -> 70.8 us (0.86)
  Pallas kernels: 76.5 us -> 65.4 us
    pallas_call x1, Pallas kernels: 76.5 us -> 65.4 us  [per_device(): pl.pallas_call(functools.partial(kernel, nx, ny, 1.0 / math.sqrt(cells)),...]
where the time goes in v3:
time: 70.8 us; the launch traced here: 70.6 us
  Pallas kernels  65.4 us (92%)
  local copies, waits for them, and re-layouts  4.54 us (6%)
    pallas_call x1, Pallas kernels, per_device(): pl.pallas_call(functools.partial(kernel, nx, ny, 1.0 / math.sqrt(cells)),...  65.4 us
    unnamed x1, local copies, waits for them, and re-layouts  3.22 us

profile of v3, /device:TPU:0, one launch (start us, length us, event | category | flops | bytes accessed | tf_op | source)
XLA Modules:
  0.0 70.6 jit_solution(7148432798001816566)
XLA Ops:
  0.6 65.4 %shard_map.68 = (f32[9,512,128]{2,1,0:T(8,128)}, f32[16,128]{1,0:T(8,128)}) custom-call(f32[9,512,128]{2,1,0:T(8,128)} %bitcast.7, s32[512,128]{1,0:T(8,128)} %bitcast.8, s32[512,128]{1,0:T(8,128)} %bitcast.9, s32[512,128]{1,0:T(8,128)} %bitcast.10, s32[512,128]{1,0:T(8,128)} %bitcast.11), custom_call_target="tpu_custom_call" | custom-call | tf_op jit(solution)/shard_map/pallas_call | solution.py:400
  66.1 1.3 %slice_reduce_fusion = f32[9]{0:T(128)} fusion(f32[16,128]{1,0:T(8,128)} %get-tuple-element.5), kind=kLoop, calls=%fused_computation | loop fusion | bytes 72 | tf_op jit(solution)/shard_map/slice | solution.py:423
  67.4 3.2 %copy.8 = f32[9,32,16,128]{3,2,1,0:T(8,128)} copy(f32[9,32,16,128]{3,2,1,0:T(8,128)} %bitcast.6) | data formatting | bytes 4718592
